TPU v7x, 32 devices: a whole 2x2x4 slice. The times are simulated.
32 devices in a mesh: tp: 2 (over y), req: 16 (over z, x, core).
Axes of the slice: x: 2, y: 2, z: 4, core: 2. Of those that a mesh axis runs over, the one named last changes fastest.
Arguments:
- token_ids: int32 [8192], P('req'), may hold values from 0 to 31999, as said below
- prompt_lengths: int32 [16, 4], P('req'), may hold values from 1 to 256, 512 in all within a row
- tenant_ids: int32 [16, 4], P('req'), may hold values from 0 to 1, never falling along the last dimension, each value on 1 to 3 neighbouring positions
- embed_table: bfloat16 [32000, 1536], P('req'), may hold values from -6 to 6
- attention_gain: float32 [1536], replicated, may hold values from 0.1 to 1.9
- qkv_weight: float32 [1536, 3072], P(('tp', 'req')), may hold values from -0.25 to 0.25
- out_weight: bfloat16 [1536, 1536], P('tp'), may hold values from -0.15625 to 0.15625
- ffn_gain: float32 [1536], replicated, may hold values from 0.1 to 1.9
- gate_up_weight: float32 [1536, 8192], P(('tp', 'req')), may hold values from -0.15625 to 0.15625
- down_weight: bfloat16 [4096, 1536], P('tp'), may hold values from -0.09375 to 0.09375
Outputs:
- final_hidden: bfloat16 [8192, 1536], P('req')
- kv_cache: bfloat16 [2, 8192, 768], P(None, 'req', 'tp')
Inputs may be any that keep to these rules, and one draw needn't show every extreme that they name: Split token_ids into aligned blocks of 256 tokens and the ids into ranges of 2000 consecutive ids: no block has more than 32 ids in one range, and one range gets exactly 32 ids from every block. `prompt_lengths`: the 4 lengths of a request group sum to 512. `tenant_ids`: never falling along the prompts of a request group; every tenant has one to 3 prompts.
All inputs are finite; a program needn't handle non-finite values.
Results may differ from a plain program's by a relative error of at most 0.01.
Values may be sent and summed in bfloat16 or wider, within the bound.
No kernel may reach another device: no remote copies, remote signals or barrier semaphores. Data moves between devices by JAX's collectives and lax.ppermute only.
A program may use at most 128 MiB of HBM per device.

v0:
```python
import jax
import jax.numpy as jnp
from jax import lax
from jax.sharding import PartitionSpec as P

HEAD_DIM = 96
rope_base = 100000.0
norm_eps = 1e-05


def rms_scaled(values, gain):
    mean_square = jnp.mean(values * values, axis=-1, keepdims=True)
    return (values * lax.rsqrt(mean_square + norm_eps) * gain).astype(jnp.bfloat16)


def token_layout(lengths, tenants, row_count):
    positions = jnp.arange(row_count, dtype=jnp.int32)
    prompt_ends = jnp.cumsum(lengths)
    prompt_starts = prompt_ends - lengths
    passed = (positions[:, None] >= prompt_ends[None, :]).astype(jnp.int32)
    prompt = jnp.sum(passed, axis=1)
    in_prompt = (prompt[:, None] == jnp.arange(lengths.shape[0], dtype=jnp.int32)[None, :]).astype(
        jnp.int32
    )
    offset = positions - jnp.sum(in_prompt * prompt_starts[None, :], axis=1)
    tenant = jnp.sum(in_prompt * tenants[None, :], axis=1)
    return (offset, tenant)


def rotate(values, offset):
    half_dim = values.shape[-1] // 2
    frequency = rope_base ** (-2.0 * jnp.arange(half_dim, dtype=jnp.float32) / values.shape[-1])
    angles = offset.astype(jnp.float32)[:, None] * frequency[None, :]
    cosine = jnp.cos(angles)[:, None, :]
    sine_part = jnp.sin(angles)[:, None, :]
    lower_half = values[..., :half_dim]
    upper_half = values[..., half_dim:]
    return jnp.concatenate(
        [
            lower_half * cosine - upper_half * sine_part,
            upper_half * cosine + lower_half * sine_part,
        ],
        axis=-1,
    )


def attend(queries, key_heads, value_heads, tenant):
    row_count = queries.shape[0]
    positions = jnp.arange(row_count, dtype=jnp.int32)
    score_scale = queries.shape[-1] ** (-0.5)
    allowed = (positions[None, :] <= positions[:, None]) & (tenant[None, :] == tenant[:, None])
    scores = (
        jnp.einsum("qkgd,skd->kgqs", queries, key_heads, preferred_element_type=jnp.float32)
        * score_scale
    )
    scores = jnp.where(allowed[None, None], scores, -jnp.inf)
    row_max = jnp.max(scores, axis=-1, keepdims=True)
    expo = jnp.exp(scores - row_max)
    weights = (expo / jnp.sum(expo, axis=-1, keepdims=True)).astype(jnp.bfloat16)
    mixed_out = jnp.einsum(
        "kgqs,skd->qkgd", weights, value_heads, preferred_element_type=jnp.float32
    )
    pieces = mixed_out.astype(jnp.bfloat16)
    return pieces


def ffn_hidden(normed_ffn, gate_cols, ff_half):
    gate_up = jnp.dot(normed_ffn, gate_cols, preferred_element_type=jnp.float32)
    return (jax.nn.silu(gate_up[:, :ff_half]) * gate_up[:, ff_half:]).astype(jnp.bfloat16)


def per_device(
    token_ids,
    prompt_lengths,
    tenant_ids,
    embed_table,
    attention_gain,
    qkv_weight,
    out_weight,
    ffn_gain,
    gate_up_weight,
    down_weight,
):
    tp_count = lax.axis_size("tp")
    tp_index = lax.axis_index("tp")
    group_count = lax.axis_size("req")
    tokens = token_ids.shape[0]
    looked = tokens // tp_count
    own_rows = embed_table.shape[0]
    capacity = max(2, 2 * looked // group_count)
    my_ids = lax.dynamic_slice_in_dim(token_ids, tp_index * looked, looked)
    owner_of = my_ids // own_rows
    row_in_range = my_ids - owner_of * own_rows
    owner_hits = (owner_of[:, None] == jnp.arange(group_count, dtype=jnp.int32)[None, :]).astype(
        jnp.int32
    )
    slot_of = jnp.sum((jnp.cumsum(owner_hits, axis=0) - owner_hits) * owner_hits, axis=1)
    requests = (
        jnp.full((group_count, capacity), -1, jnp.int32).at[owner_of, slot_of].set(row_in_range)
    )
    found_rows = jnp.take(
        embed_table,
        jnp.maximum(lax.all_to_all(requests, "req", split_axis=0, concat_axis=0, tiled=True), 0),
        axis=0,
    )
    returned = lax.all_to_all(found_rows, "req", split_axis=0, concat_axis=0, tiled=True)
    embedded = lax.all_gather(returned[owner_of, slot_of], "tp", axis=0, tiled=True)
    offset, tenant = token_layout(prompt_lengths[0], tenant_ids[0], tokens)
    rows_here = qkv_weight.shape[0]
    q_half = out_weight.shape[0]
    ff_half = down_weight.shape[0]
    q_full = q_half * tp_count
    kv_half = (qkv_weight.shape[1] - q_full) // (2 * tp_count)
    kv_full = kv_half * tp_count
    packed = qkv_weight.astype(jnp.bfloat16)
    gate_up_bf = gate_up_weight.astype(jnp.bfloat16)
    packed_rows = jnp.concatenate(
        [
            packed[:, :q_full].reshape(rows_here, tp_count, q_half),
            packed[:, q_full : q_full + kv_full].reshape(rows_here, tp_count, kv_half),
            packed[:, q_full + kv_full :].reshape(rows_here, tp_count, kv_half),
            gate_up_bf.reshape(rows_here, 2, tp_count, ff_half)
            .transpose(0, 2, 1, 3)
            .reshape(rows_here, tp_count, 2 * ff_half),
        ],
        axis=2,
    )
    collected = lax.all_gather(packed_rows, "req", axis=0, tiled=True)
    columns = lax.all_to_all(collected, "tp", split_axis=1, concat_axis=0, tiled=True)
    weights = columns[:, 0, :]
    normed = rms_scaled(embedded.astype(jnp.float32), attention_gain)
    projected = jnp.dot(
        normed, weights[:, : q_half + 2 * kv_half], preferred_element_type=jnp.float32
    )
    kv_local = kv_half // HEAD_DIM
    queries = rotate(
        projected[:, :q_half].reshape(tokens, q_half // HEAD_DIM, HEAD_DIM), offset
    ).astype(jnp.bfloat16)
    key_heads = rotate(
        projected[:, q_half : q_half + kv_half].reshape(tokens, kv_local, HEAD_DIM), offset
    ).astype(jnp.bfloat16)
    value_heads = (
        projected[:, q_half + kv_half :].reshape(tokens, kv_local, HEAD_DIM).astype(jnp.bfloat16)
    )
    kv_cache = jnp.stack([key_heads.reshape(tokens, kv_half), value_heads.reshape(tokens, kv_half)])
    attended = attend(
        queries.reshape(tokens, kv_local, -1, HEAD_DIM), key_heads, value_heads, tenant
    ).reshape(tokens, q_half)
    gate_cols = weights[:, q_half + 2 * kv_half :]
    attn_sum = lax.psum(
        jnp.dot(attended, out_weight, preferred_element_type=jnp.float32).astype(jnp.bfloat16), "tp"
    ).astype(jnp.float32)
    residual = embedded.astype(jnp.float32) + attn_sum
    normed_ffn = rms_scaled(residual, ffn_gain)
    hidden = ffn_hidden(normed_ffn, gate_cols, ff_half)
    ffn_sum = lax.psum(
        jnp.dot(hidden, down_weight, preferred_element_type=jnp.float32).astype(jnp.bfloat16), "tp"
    ).astype(jnp.float32)
    final_out = (residual + ffn_sum).astype(jnp.bfloat16)
    return (final_out, kv_cache)


def solution(mesh):
    return jax.shard_map(
        per_device,
        mesh=mesh,
        in_specs=(
            P("req"),
            P("req", None),
            P("req", None),
            P("req", None),
            P(),
            P(("tp", "req"), None),
            P("tp", None),
            P(),
            P(("tp", "req"), None),
            P("tp", None),
        ),
        out_specs=(P("req", None), P(None, "req", "tp")),
        check_vma=False,
    )
```

profile of v0, /device:TPU:0, one launch (start us, length us, event | category | flops | bytes accessed | tf_op | source)
XLA Modules:
  0.0 530.0 jit_solution(3900098590027576408)
XLA Ops:
  8.1 1.2 convert_element_type.91
  9.3 2.4 convert_element_type.92
  11.7 2.6 reshape.236
  14.3 1.5 copy.85
  15.8 2.5 reshape.237
  20.5 12.8 %scatter_fusion = s32[16,32]{1,0:T(8,128)S(1)} fusion(s32[16,32]{1,0:T(8,128)S(1)} %broadcast_in_dim.22, s32[256]{0:T(256)S(1)} %bitcast.107, s32[256]{0:T(256)S(1)} %get-tuple-element.4), kind=kCustom, calls=%fused_computation.2 | custom fusion | bytes 5120 | tf_op jit(solution)/shard_map/scatter | solution.py:99
  33.3 13.7 %all_to_all.29 = s32[16,1,32]{2,1,0:T(1,128)S(1)} all-to-all(s32[16,1,32]{2,1,0:T(1,128)S(1)} %bitcast.105), channel_id=1, replica_groups=mesh['tp'=2,'req'=16] {'req'}, dimensions={0} | all-to-all | bytes 4096 | tf_op jit(solution)/shard_map/all_to_all | solution.py:103
  47.0 8.0 %gather_fusion = bf16[512,1536]{1,0:T(8,128)(2,1)} fusion(bf16[2000,1536]{1,0:T(8,128)(2,1)} %param.13, s32[1024]{0:T(1024)S(1)} %pad_clamp_fusion), kind=kCustom, calls=%fused_computation | custom fusion | bytes 3147776 | tf_op jit(solution)/shard_map/jit(_take)/gather | solution.py:101
  55.0 1.7 broadcast_select_fusion
  56.7 60.0 %all_to_all.30 = bf16[16,32,1536]{2,1,0:T(8,128)(2,1)} all-to-all(bf16[16,32,1536]{2,1,0:T(8,128)(2,1)S(1)} %broadcast_select_fusion), channel_id=1, replica_groups=mesh['tp'=2,'req'=16] {'req'}, dimensions={0} | all-to-all | bytes 3145728 | tf_op jit(solution)/shard_map/all_to_all | solution.py:106
  116.7 25.0 %all-gather.5.cloned.1.call-done = bf16[768,2,5632]{2,0,1:T(8,128)(2,1)} async-done(((bf16[48,2,5632]{2,0,1:T(8,128)(2,1)}), bf16[768,2,5632]{2,0,1:T(8,128)(2,1)}) %all-gather.5.cloned.1.call-update) | async-done | bytes 17301520 | tf_op jit(solution)/shard_map/all_gather | solution.py:128
  141.7 9.8 %all-to-all-start.2 = ((bf16[768,2,5632]{2,0,1:T(8,128)(2,1)}), bf16[768,2,5632]{2,0,1:T(8,128)(2,1)}, u32[]{:S(2)}, u32[]{:S(2)}) async-start(bf16[768,2,5632]{2,0,1:T(8,128)(2,1)} %all-gather.5.cloned.1.call-done), calls=%async_computation.2 | async-start | bytes 34603008 | tf_op jit(solution)/shard_map/all_to_all | solution.py:129
  151.6 4.6 gather_fusion.1
  158.9 47.1 %all-gather.3.cloned.1.call-done = bf16[512,1536]{1,0:T(8,128)(2,1)} async-done(((bf16[256,1536]{1,0:T(8,128)(2,1)}), bf16[512,1536]{1,0:T(8,128)(2,1)}) %all-gather.3.cloned.1.call-update) | async-done | bytes 1572880 | tf_op jit(solution)/shard_map/all_gather | solution.py:107
  206.0 1.8 fusion.11
  207.8 149.1 %all-to-all-done.2 = bf16[768,2,5632]{2,0,1:T(8,128)(2,1)} async-done(((bf16[768,2,5632]{2,0,1:T(8,128)(2,1)}), bf16[768,2,5632]{2,0,1:T(8,128)(2,1)}, u32[]{:S(2)}, u32[]{:S(2)}) %all-to-all-start.2) | async-done | bytes 17301536 | tf_op jit(solution)/shard_map/all_to_all | solution.py:129
  356.9 5.0 fusion.4
  362.0 1.4 slice.79
  365.1 3.1 copy.70
  368.3 1.1 copy.69
  369.5 2.4 subtract_convert_fusion
  371.8 1.2 multiply_subtract_fusion
  373.1 7.4 %fusion.44 = (f32[4,2,512]{2,1,0:T(2,128)S(1)}, f32[4,2,512,512]{2,3,1,0:T(8,128)}) fusion(pred[512,512]{0,1:T(8,128)(4,1)} %fusion.21, bf16[512,4,2,48]{0,3,2,1:T(8,128)(2,1)} %bitcast.117, bf16[512,4,2,48]{0,3,2,1:T(8,128)(2,1)S(1)} %bitcast.116, bf16[512,4,48]{0,2,1:T(8,128)(2,1)S(1)} %get-tuple-element.11, bf16[512,4,48]{0,2,1:T(8,128)(2,1)S(1)} %get-tuple-element.10), kind=kOutput, calls=%fused_computation.93 | convolution fusion | flops 413401600 | bytes 9846784 | tf_op jit(solution)/shard_map/sub | solution.py:58
  380.5 4.2 fusion.20
  384.7 2.6 convolution_convert_fusion.1
  387.6 55.3 %all-reduce.3.cloned.1.call-done = bf16[512,1536]{1,0:T(8,128)(2,1)} async-done(((bf16[512,1536]{1,0:T(8,128)(2,1)}), bf16[512,1536]{1,0:T(8,128)(2,1)}) %all-reduce.3.cloned.1.call-update) | async-done | bytes 1572880 | tf_op jit(solution)/shard_map/psum | solution.py:150
  442.9 2.6 multiply_reduce_fusion
  445.7 12.1 %fusion.1 = f32[512,4096]{1,0:T(8,128)} fusion(bf16[1536,5632]{1,0:T(8,128)(2,1)} %bitcast.14, bf16[512,1536]{1,0:T(8,128)(2,1)S(1)} %copy-done.2, bf16[512,1536]{1,0:T(8,128)(2,1)S(1)} %copy-done.1, f32[1536]{0:T(1024)S(1)} %copy-done.10, f32[512]{0:T(512)S(1)} %add_rsqrt_fusion), kind=kOutput, calls=%fused_computation.4 | convolution fusion | flops 6447169536 | bytes 24125440 | tf_op jit(solution)/shard_map/dot_general | solution.py:68
  457.8 9.1 %convolution_convert_fusion = bf16[512,1536]{1,0:T(8,128)(2,1)} fusion(bf16[2048,1536]{1,0:T(8,128)(2,1)S(1)} %bitcast.129, f32[512,4096]{1,0:T(8,128)} %fusion.1), kind=kOutput, calls=%fused_computation.27 | convolution fusion | flops 3228303360 | bytes 16252928 | tf_op jit(solution)/shard_map/dot_general | solution.py:157
  467.2 1.2 slice_bitcast_fusion
  469.4 49.0 %all-reduce.5.cloned.1.call-done = bf16[512,1536]{1,0:T(8,128)(2,1)} async-done(((bf16[512,1536]{1,0:T(8,128)(2,1)}), bf16[512,1536]{1,0:T(8,128)(2,1)}) %all-reduce.5.cloned.1.call-update) | async-done | bytes 1572880 | tf_op jit(solution)/shard_map/psum | solution.py:156
  518.3 4.1 add_convert_fusion
  (73 shorter events, 8.5 us)
Async XLA Ops:
  8.0 376.7 %copy-start = (bf16[768,1536]{1,0:T(8,128)(2,1)S(1)}, bf16[768,1536]{1,0:T(8,128)(2,1)}, u32[]{:S(2)}) copy-start(bf16[768,1536]{1,0:T(8,128)(2,1)} %param.16) | copy-start | bytes 7077892
  8.0 133.7 %all-gather.5.cloned.1.call-start = ((), (), s32[]{:S(2)}) async-start(), calls=%async_computation.4 | async-start | bytes 18382848 | tf_op jit(solution)/shard_map/all_gather | solution.py:128
  14.3 5.2 copy-start.8
  141.7 215.2 %all-to-all-start.2 = ((bf16[768,2,5632]{2,0,1:T(8,128)(2,1)}), bf16[768,2,5632]{2,0,1:T(8,128)(2,1)}, u32[]{:S(2)}, u32[]{:S(2)}) async-start(bf16[768,2,5632]{2,0,1:T(8,128)(2,1)} %all-gather.5.cloned.1.call-done), calls=%async_computation.2 | async-start | bytes 34603008 | tf_op jit(solution)/shard_map/all_to_all | solution.py:129
  151.5 54.5 %all-gather.3.cloned.1.call-start = ((), (), s32[]{:S(2)}) async-start(), calls=%async_computation.3 | async-start | bytes 2359296 | tf_op jit(solution)/shard_map/all_gather | solution.py:107
  151.6 4.9 copy-start.11
  151.6 5.2 copy-start.7
  151.6 205.3 %copy-start.9 = (f32[1536]{0:T(1024)S(1)}, f32[1536]{0:T(1024)}, u32[]{:S(2)}) copy-start(f32[1536]{0:T(1024)} %param.14) | copy-start | bytes 18436
  156.3 286.6 %all-reduce.3.cloned.1.call-start = ((), (), s32[]{:S(2)}) async-start(), calls=%async_computation.5 | async-start | bytes 3145728 | tf_op jit(solution)/shard_map/psum | solution.py:150
  362.0 2.2 copy-start.3
  364.2 4.1 slice-start
  365.1 4.3 copy-start.4
  365.1 4.3 copy-start.5
  373.1 7.4 %copy-start.6 = (bf16[512,384]{0,1:T(8,128)(2,1)S(1)}, bf16[512,384]{0,1:T(8,128)(2,1)}, u32[]{:S(2)}) copy-start(bf16[512,384]{0,1:T(8,128)(2,1)} %copy.68) | copy-start | bytes 1179652
  387.3 58.3 %copy-start.10 = (f32[1536]{0:T(1024)S(1)}, f32[1536]{0:T(1024)}, u32[]{:S(2)}) copy-start(f32[1536]{0:T(1024)} %param.17) | copy-start | bytes 18436
  387.3 131.0 %all-reduce.5.cloned.1.call-start = ((), (), s32[]{:S(2)}) async-start(), calls=%async_computation.6 | async-start | bytes 3145728 | tf_op jit(solution)/shard_map/psum | solution.py:156
  442.9 2.6 copy-start.1
  442.9 2.8 copy-start.2
  442.9 14.9 %slice-start.1 = ((s8[6291456]{0:T(1024)(128)(4,1)}), s8[4194304]{0:T(1024)(128)(4,1)S(1)}, s32[]{:S(2)}) async-start(s8[6291456]{0:T(1024)(128)(4,1)} %bitcast.128), calls=%async_computation.8 | async-start | bytes 8388608
  445.7 12.1 %slice-start.2 = ((s8[6291456]{0:T(1024)(128)(4,1)}), s8[2097152]{0:T(1024)(128)(4,1)S(1)}, s32[]{:S(2)}) async-start(s8[6291456]{0:T(1024)(128)(4,1)} %bitcast.128), calls=%async_computation.9 | async-start | bytes 4194304
Sparse Core Ops, SparseCore 0:
  19.6 122.0 all-gather.4
Sparse Core Ops, SparseCore 1:
  156.4 49.6 all-gather.2
  387.4 55.5 all-reduce.2
  467.0 51.2 all-reduce.4
where the time goes:
time: 531 us; the launch traced here: 530 us
  waiting for transfers between devices  325 us (61%)
  blocking collectives  73.7 us (14%)
  local copies, waits for them, and re-layouts  41.4 us (8%)
  matrix products  40.4 us (8%)
  other arithmetic  22.7 us (4%)
  between operations  15.9 us (3%)
  starting transfers between devices  10.4 us (2%)
    all_to_all x1, waiting for transfers between devices, per_device(): lax.all_to_all(collected, 'tp', split_axis=1, concat_axis=0, tiled=True)  149 us
    all_to_all x1, blocking collectives, per_device(): lax.all_to_all(found_rows, 'req', split_axis=0, concat_axis=0, tiled=True)  60 us
    psum x1, waiting for transfers between devices, per_device(): lax.psum(jnp.dot(attended, out_weight, preferred_element_type=jnp.float32...  55.3 us
    psum x1, waiting for transfers between devices, per_device(): lax.psum(jnp.dot(hidden, down_weight, preferred_element_type=jnp.float32)...  49 us
    all_gather x1, waiting for transfers between devices, per_device(): lax.all_gather(returned[owner_of, slot_of], 'tp', axis=0, tiled=True)  47.1 us
    all_gather x1, waiting for transfers between devices, per_device(): collected = lax.all_gather(packed_rows, 'req', axis=0, tiled=True)  25 us
    all_to_all x1, blocking collectives, per_device(): lax.all_to_all(requests, 'req', split_axis=0, concat_axis=0, tiled=True)  13.7 us
    scatter x1, local copies, waits for them, and re-layouts, per_device(): jnp.full((group_count, capacity), -1, jnp.int32).at[owner_of, slot_of]  12.8 us
  transfers between devices with their start and end apart: 5, of which 5 were waited for; matrix products, arithmetic and copies ran while one was open for 7% of the time, Pallas kernels for 0%

commit v1 on v0

--- a/solution.py
+++ b/solution.py
@@ -6,6 +6,30 @@
 HEAD_DIM = 96
 rope_base = 100000.0
 norm_eps = 1e-05
+
+
+def split_up(array, dim, size):
+    lengths = array.shape
+    parts = array.reshape(*lengths[:dim], size, lengths[dim] // size, *lengths[dim + 1 :])
+    return jnp.moveaxis(parts, dim, 0)
+
+
+def laid_out(tiles, dim):
+    tiles = jnp.moveaxis(tiles, 0, dim)
+    dims = tiles.shape
+    return tiles.reshape(*dims[:dim], dims[dim] * dims[dim + 1], *dims[dim + 2 :])
+
+
+def exchange_directly(x, axis, split_dim, concat_dim):
+    size, index = (lax.axis_size(axis), lax.axis_index(axis))
+    blocks = split_up(x, split_dim, size)
+    out = blocks
+    for step in range(1, size):
+        target, source = ((index + step) % size, (index - step) % size)
+        sent = lax.dynamic_index_in_dim(blocks, target, 0)
+        other = lax.ppermute(sent, axis, [(i, (i + step) % size) for i in range(size)])
+        out = lax.dynamic_update_slice_in_dim(out, other, source, axis=0)
+    return laid_out(out, concat_dim)
 
 
 def rms_scaled(values, gain):
@@ -99,9 +123,7 @@
         jnp.full((group_count, capacity), -1, jnp.int32).at[owner_of, slot_of].set(row_in_range)
     )
     found_rows = jnp.take(
-        embed_table,
-        jnp.maximum(lax.all_to_all(requests, "req", split_axis=0, concat_axis=0, tiled=True), 0),
-        axis=0,
+        embed_table, jnp.maximum(exchange_directly(requests, "req", 0, 0), 0), axis=0
     )
     returned = lax.all_to_all(found_rows, "req", split_axis=0, concat_axis=0, tiled=True)
     embedded = lax.all_gather(returned[owner_of, slot_of], "tp", axis=0, tiled=True)

time: 531 us -> 531 us (level)
  starting transfers between devices: 10.4 us -> 35 us
  waiting for transfers between devices: 325 us -> 311 us
  blocking collectives: 73.7 us -> 62.3 us
    ppermute x0 -> x15, starting transfers between devices: none -> 24.5 us  [exchange_directly(): lax.ppermute(sent, axis, [(i, (i + step) % size) for i in range(size)])]
    all_gather x1, waiting for transfers between devices: 25 us -> 9.8 us  [per_device(): collected = lax.all_gather(packed_rows, 'req', axis=0, tiled=True)]
    all_to_all x1 -> x0, blocking collectives: 13.7 us -> none  [per_device(): lax.all_to_all(requests, 'req', split_axis=0, concat_axis=0, tiled=True)]
  transfers between devices with their start and end apart: 5 -> 20, of which waited for: 5 -> 6; matrix products, arithmetic and copies ran while one was open for 7% -> 7% of each run, Pallas kernels for 0% -> 0%
where the time goes in v1:
time: 531 us; the launch traced here: 530 us
  waiting for transfers between devices  311 us (59%)
  blocking collectives  62.3 us (12%)
  local copies, waits for them, and re-layouts  42 us (8%)
  matrix products  40.3 us (8%)
  starting transfers between devices  35 us (7%)
  other arithmetic  22.6 us (4%)
  between operations  16.2 us (3%)
    all_to_all x1, waiting for transfers between devices, per_device(): lax.all_to_all(collected, 'tp', split_axis=1, concat_axis=0, tiled=True)  149 us
    all_to_all x1, blocking collectives, per_device(): lax.all_to_all(found_rows, 'req', split_axis=0, concat_axis=0, tiled=True)  62.3 us
    psum x1, waiting for transfers between devices, per_device(): lax.psum(jnp.dot(attended, out_weight, preferred_element_type=jnp.float32...  55.3 us
    psum x1, waiting for transfers between devices, per_device(): lax.psum(jnp.dot(hidden, down_weight, preferred_element_type=jnp.float32)...  49 us
    all_gather x1, waiting for transfers between devices, per_device(): lax.all_gather(returned[owner_of, slot_of], 'tp', axis=0, tiled=True)  47.1 us
    ppermute x15, starting transfers between devices, exchange_directly(): lax.ppermute(sent, axis, [(i, (i + step) % size) for i in range(size)])  24.5 us
    scatter x1, local copies, waits for them, and re-layouts, per_device(): jnp.full((group_count, capacity), -1, jnp.int32).at[owner_of, slot_of]  12.8 us
    dot_general x1, matrix products, ffn_hidden(): gate_up = jnp.dot(normed_ffn, gate_cols, preferred_element_type=jnp.float32)  12 us
  transfers between devices with their start and end apart: 20, of which 6 were waited for; matrix products, arithmetic and copies ran while one was open for 7% of the time, Pallas kernels for 0%

profile of v1, /device:TPU:0, one launch (start us, length us, event | category | flops | bytes accessed | tf_op | source)
XLA Modules:
  0.0 529.9 jit_solution(1350788178939315881)
XLA Ops:
  9.3 2.4 convert_element_type.92
  11.7 2.6 reshape.310
  15.8 2.5 reshape.311
  20.7 12.8 %scatter_fusion = s32[16,32]{1,0:T(8,128)S(1)} fusion(s32[16,32]{1,0:T(8,128)S(1)} %broadcast_in_dim.24, s32[256]{0:T(256)S(1)} %bitcast.143, s32[256]{0:T(256)S(1)} %get-tuple-element.4), kind=kCustom, calls=%fused_computation.2 | custom fusion | bytes 5120 | tf_op jit(solution)/shard_map/scatter | solution.py:123
  34.1 2.6 collective-permute-start.1
  36.7 2.4 collective-permute-start.2
  42.1 4.4 collective-permute-start.6
  47.3 2.4 collective-permute-start.9
  49.7 2.9 collective-permute-start.10
  52.7 1.9 collective-permute-start.11
  56.2 2.3 collective-permute-start.14
  59.9 8.1 %gather_fusion = bf16[512,1536]{1,0:T(8,128)(2,1)} fusion(bf16[2000,1536]{1,0:T(8,128)(2,1)} %param.13, s32[1024]{0:T(1024)S(1)} %pad_clamp_fusion), kind=kCustom, calls=%fused_computation | custom fusion | bytes 3147776 | tf_op jit(solution)/shard_map/jit(_take)/gather | solution.py:125
  68.0 1.6 broadcast_select_fusion
  69.6 62.3 %all_to_all.20 = bf16[16,32,1536]{2,1,0:T(8,128)(2,1)} all-to-all(bf16[16,32,1536]{2,1,0:T(8,128)(2,1)S(1)} %broadcast_select_fusion), channel_id=1, replica_groups=mesh['tp'=2,'req'=16] {'req'}, dimensions={0} | all-to-all | bytes 3145728 | tf_op jit(solution)/shard_map/all_to_all | solution.py:128
  131.9 9.8 %all-gather.5.cloned.1.call-done = bf16[768,2,5632]{2,0,1:T(8,128)(2,1)} async-done(((bf16[48,2,5632]{2,0,1:T(8,128)(2,1)}), bf16[768,2,5632]{2,0,1:T(8,128)(2,1)}) %all-gather.5.cloned.1.call-update) | async-done | bytes 17301520 | tf_op jit(solution)/shard_map/all_gather | solution.py:150
  141.7 9.9 %all-to-all-start.1 = ((bf16[768,2,5632]{2,0,1:T(8,128)(2,1)}), bf16[768,2,5632]{2,0,1:T(8,128)(2,1)}, u32[]{:S(2)}, u32[]{:S(2)}) async-start(bf16[768,2,5632]{2,0,1:T(8,128)(2,1)} %all-gather.5.cloned.1.call-done), calls=%async_computation.1 | async-start | bytes 34603008 | tf_op jit(solution)/shard_map/all_to_all | solution.py:151
  151.8 4.7 gather_fusion.1
  159.0 47.1 %all-gather.3.cloned.1.call-done = bf16[512,1536]{1,0:T(8,128)(2,1)} async-done(((bf16[256,1536]{1,0:T(8,128)(2,1)}), bf16[512,1536]{1,0:T(8,128)(2,1)}) %all-gather.3.cloned.1.call-update) | async-done | bytes 1572880 | tf_op jit(solution)/shard_map/all_gather | solution.py:129
  206.1 1.8 fusion.11
  207.9 149.1 %all-to-all-done.1 = bf16[768,2,5632]{2,0,1:T(8,128)(2,1)} async-done(((bf16[768,2,5632]{2,0,1:T(8,128)(2,1)}), bf16[768,2,5632]{2,0,1:T(8,128)(2,1)}, u32[]{:S(2)}, u32[]{:S(2)}) %all-to-all-start.1) | async-done | bytes 17301536 | tf_op jit(solution)/shard_map/all_to_all | solution.py:151
  357.0 5.0 fusion.4
  365.2 3.2 copy.45
  369.5 2.4 subtract_convert_fusion
  373.1 7.4 %fusion.59 = (f32[4,2,512]{2,1,0:T(2,128)S(1)}, f32[4,2,512,512]{2,3,1,0:T(8,128)}) fusion(pred[512,512]{0,1:T(8,128)(4,1)} %fusion.21, bf16[512,4,2,48]{0,3,2,1:T(8,128)(2,1)} %bitcast.153, bf16[512,4,2,48]{0,3,2,1:T(8,128)(2,1)S(1)} %bitcast.152, bf16[512,4,48]{0,2,1:T(8,128)(2,1)S(1)} %get-tuple-element.11, bf16[512,4,48]{0,2,1:T(8,128)(2,1)S(1)} %get-tuple-element.10), kind=kOutput, calls=%fused_computation.123 | convolution fusion | flops 413401600 | bytes 9846784 | tf_op jit(solution)/shard_map/sub | solution.py:82
  380.5 4.2 fusion.20
  384.7 2.6 convolution_convert_fusion.1
  387.6 55.3 %all-reduce.3.cloned.1.call-done = bf16[512,1536]{1,0:T(8,128)(2,1)} async-done(((bf16[512,1536]{1,0:T(8,128)(2,1)}), bf16[512,1536]{1,0:T(8,128)(2,1)}) %all-reduce.3.cloned.1.call-update) | async-done | bytes 1572880 | tf_op jit(solution)/shard_map/psum | solution.py:172
  442.9 2.6 multiply_reduce_fusion
  445.7 12.0 %fusion.1 = f32[512,4096]{1,0:T(8,128)} fusion(bf16[1536,5632]{1,0:T(8,128)(2,1)} %bitcast.40, bf16[512,1536]{1,0:T(8,128)(2,1)S(1)} %copy-done.2, bf16[512,1536]{1,0:T(8,128)(2,1)S(1)} %copy-done.1, f32[1536]{0:T(1024)S(1)} %copy-done.10, f32[512]{0:T(512)S(1)} %add_rsqrt_fusion), kind=kOutput, calls=%fused_computation.4 | convolution fusion | flops 6447169536 | bytes 24125440 | tf_op jit(solution)/shard_map/dot_general | solution.py:92
  457.7 9.1 %convolution_convert_fusion = bf16[512,1536]{1,0:T(8,128)(2,1)} fusion(bf16[2048,1536]{1,0:T(8,128)(2,1)S(1)} %bitcast.178, f32[512,4096]{1,0:T(8,128)} %fusion.1), kind=kOutput, calls=%fused_computation.27 | convolution fusion | flops 3228303360 | bytes 16252928 | tf_op jit(solution)/shard_map/dot_general | solution.py:179
  469.3 49.0 %all-reduce.5.cloned.1.call-done = bf16[512,1536]{1,0:T(8,128)(2,1)} async-done(((bf16[512,1536]{1,0:T(8,128)(2,1)}), bf16[512,1536]{1,0:T(8,128)(2,1)}) %all-reduce.5.cloned.1.call-update) | async-done | bytes 1572880 | tf_op jit(solution)/shard_map/psum | solution.py:178
  518.2 4.1 add_convert_fusion
  (118 shorter events, 23.5 us)
Async XLA Ops:
  8.0 376.7 %copy-start = (bf16[768,1536]{1,0:T(8,128)(2,1)S(1)}, bf16[768,1536]{1,0:T(8,128)(2,1)}, u32[]{:S(2)}) copy-start(bf16[768,1536]{1,0:T(8,128)(2,1)} %param.16) | copy-start | bytes 7077892
  8.0 133.6 %all-gather.5.cloned.1.call-start = ((), (), s32[]{:S(2)}) async-start(), calls=%async_computation.3 | async-start | bytes 18382848 | tf_op jit(solution)/shard_map/all_gather | solution.py:150
  15.8 3.9 copy-start.8
  33.6 7.2 %collective-permute-start = (s32[1,1,32]{2,1,0:T(1,128)S(1)}, s32[1,1,32]{2,1,0:T(1,128)S(1)}, u32[]{:S(2)}, u32[]{:S(2)}) collective-permute-start(s32[1,1,32]{2,1,0:T(1,128)S(1)} %get-tuple-element.28), channel_id=1, source_target_pairs={{0,1},{1,2},{2,3},{3,4},{4,5},{5,6},{6,7},{7,8},{8,9},{9,10},{10,1... | collective-permute-start | bytes 392 | tf_op jit(solution)/shard_map/ppermute | solution.py:30
  34.1 8.0 %collective-permute-start.1 = (s32[1,1,32]{2,1,0:T(1,128)S(1)}, s32[1,1,32]{2,1,0:T(1,128)S(1)}, u32[]{:S(2)}, u32[]{:S(2)}) collective-permute-start(s32[1,1,32]{2,1,0:T(1,128)S(1)} %get-tuple-element.27), channel_id=1, source_target_pairs={{0,2},{1,3},{2,4},{3,5},{4,6},{5,7},{6,8},{7,9},{8,10},{9,11},{10,... | collective-permute-start | bytes 392 | tf_op jit(solution)/shard_map/ppermute | solution.py:30
  36.7 9.8 %collective-permute-start.2 = (s32[1,1,32]{2,1,0:T(1,128)S(1)}, s32[1,1,32]{2,1,0:T(1,128)S(1)}, u32[]{:S(2)}, u32[]{:S(2)}) collective-permute-start(s32[1,1,32]{2,1,0:T(1,128)S(1)} %get-tuple-element.26), channel_id=1, source_target_pairs={{0,3},{1,4},{2,5},{3,6},{4,7},{5,8},{6,9},{7,10},{8,11},{9,12},{10... | collective-permute-start | bytes 392 | tf_op jit(solution)/shard_map/ppermute | solution.py:30
  39.1 7.8 %collective-permute-start.3 = (s32[1,1,32]{2,1,0:T(1,128)S(1)}, s32[1,1,32]{2,1,0:T(1,128)S(1)}, u32[]{:S(2)}, u32[]{:S(2)}) collective-permute-start(s32[1,1,32]{2,1,0:T(1,128)S(1)} %get-tuple-element.25), channel_id=1, source_target_pairs={{0,4},{1,5},{2,6},{3,7},{4,8},{5,9},{6,10},{7,11},{8,12},{9,13},{1... | collective-permute-start | bytes 392 | tf_op jit(solution)/shard_map/ppermute | solution.py:30
  40.7 6.6 %collective-permute-start.4 = (s32[1,1,32]{2,1,0:T(1,128)S(1)}, s32[1,1,32]{2,1,0:T(1,128)S(1)}, u32[]{:S(2)}, u32[]{:S(2)}) collective-permute-start(s32[1,1,32]{2,1,0:T(1,128)S(1)} %get-tuple-element.24), channel_id=1, source_target_pairs={{0,5},{1,6},{2,7},{3,8},{4,9},{5,10},{6,11},{7,12},{8,13},{9,14},{... | collective-permute-start | bytes 392 | tf_op jit(solution)/shard_map/ppermute | solution.py:30
  40.8 8.9 %collective-permute-start.5 = (s32[1,1,32]{2,1,0:T(1,128)S(1)}, s32[1,1,32]{2,1,0:T(1,128)S(1)}, u32[]{:S(2)}, u32[]{:S(2)}) collective-permute-start(s32[1,1,32]{2,1,0:T(1,128)S(1)} %get-tuple-element.23), channel_id=1, source_target_pairs={{0,6},{1,7},{2,8},{3,9},{4,10},{5,11},{6,12},{7,13},{8,14},{9,15},... | collective-permute-start | bytes 392 | tf_op jit(solution)/shard_map/ppermute | solution.py:30
  42.1 10.6 %collective-permute-start.6 = (s32[1,1,32]{2,1,0:T(1,128)S(1)}, s32[1,1,32]{2,1,0:T(1,128)S(1)}, u32[]{:S(2)}, u32[]{:S(2)}) collective-permute-start(s32[1,1,32]{2,1,0:T(1,128)S(1)} %get-tuple-element.22), channel_id=1, source_target_pairs={{0,7},{1,8},{2,9},{3,10},{4,11},{5,12},{6,13},{7,14},{8,15},{9,0},... | collective-permute-start | bytes 392 | tf_op jit(solution)/shard_map/ppermute | solution.py:30
  46.5 8.1 %collective-permute-start.7 = (s32[1,1,32]{2,1,0:T(1,128)S(1)}, s32[1,1,32]{2,1,0:T(1,128)S(1)}, u32[]{:S(2)}, u32[]{:S(2)}) collective-permute-start(s32[1,1,32]{2,1,0:T(1,128)S(1)} %get-tuple-element.21), channel_id=1, source_target_pairs={{0,8},{1,9},{2,10},{3,11},{4,12},{5,13},{6,14},{7,15},{8,0},{9,1},... | collective-permute-start | bytes 392 | tf_op jit(solution)/shard_map/ppermute | solution.py:30
  46.9 7.8 %collective-permute-start.8 = (s32[1,1,32]{2,1,0:T(1,128)S(1)}, s32[1,1,32]{2,1,0:T(1,128)S(1)}, u32[]{:S(2)}, u32[]{:S(2)}) collective-permute-start(s32[1,1,32]{2,1,0:T(1,128)S(1)} %get-tuple-element.20), channel_id=1, source_target_pairs={{0,9},{1,10},{2,11},{3,12},{4,13},{5,14},{6,15},{7,0},{8,1},{9,2},... | collective-permute-start | bytes 392 | tf_op jit(solution)/shard_map/ppermute | solution.py:30
  47.3 8.9 %collective-permute-start.9 = (s32[1,1,32]{2,1,0:T(1,128)S(1)}, s32[1,1,32]{2,1,0:T(1,128)S(1)}, u32[]{:S(2)}, u32[]{:S(2)}) collective-permute-start(s32[1,1,32]{2,1,0:T(1,128)S(1)} %get-tuple-element.19), channel_id=1, source_target_pairs={{0,10},{1,11},{2,12},{3,13},{4,14},{5,15},{6,0},{7,1},{8,2},{9,3},... | collective-permute-start | bytes 392 | tf_op jit(solution)/shard_map/ppermute | solution.py:30
  49.7 8.8 %collective-permute-start.10 = (s32[1,1,32]{2,1,0:T(1,128)S(1)}, s32[1,1,32]{2,1,0:T(1,128)S(1)}, u32[]{:S(2)}, u32[]{:S(2)}) collective-permute-start(s32[1,1,32]{2,1,0:T(1,128)S(1)} %get-tuple-element.18), channel_id=1, source_target_pairs={{0,11},{1,12},{2,13},{3,14},{4,15},{5,0},{6,1},{7,2},{8,3},{9,4},{... | collective-permute-start | bytes 392 | tf_op jit(solution)/shard_map/ppermute | solution.py:30
  52.7 5.8 %collective-permute-start.11 = (s32[1,1,32]{2,1,0:T(1,128)S(1)}, s32[1,1,32]{2,1,0:T(1,128)S(1)}, u32[]{:S(2)}, u32[]{:S(2)}) collective-permute-start(s32[1,1,32]{2,1,0:T(1,128)S(1)} %get-tuple-element.17), channel_id=1, source_target_pairs={{0,12},{1,13},{2,14},{3,15},{4,0},{5,1},{6,2},{7,3},{8,4},{9,5},{1... | collective-permute-start | bytes 392 | tf_op jit(solution)/shard_map/ppermute | solution.py:30
  54.6 4.0 collective-permute-start.12
  54.7 3.9 collective-permute-start.13
  56.2 3.6 collective-permute-start.14
  141.7 215.3 %all-to-all-start.1 = ((bf16[768,2,5632]{2,0,1:T(8,128)(2,1)}), bf16[768,2,5632]{2,0,1:T(8,128)(2,1)}, u32[]{:S(2)}, u32[]{:S(2)}) async-start(bf16[768,2,5632]{2,0,1:T(8,128)(2,1)} %all-gather.5.cloned.1.call-done), calls=%async_computation.1 | async-start | bytes 34603008 | tf_op jit(solution)/shard_map/all_to_all | solution.py:151
  151.6 54.5 %all-gather.3.cloned.1.call-start = ((), (), s32[]{:S(2)}) async-start(), calls=%async_computation.2 | async-start | bytes 2359296 | tf_op jit(solution)/shard_map/all_gather | solution.py:129
  151.8 4.8 copy-start.11
  151.8 5.0 copy-start.7
  151.8 205.1 %copy-start.9 = (f32[1536]{0:T(1024)S(1)}, f32[1536]{0:T(1024)}, u32[]{:S(2)}) copy-start(f32[1536]{0:T(1024)} %param.14) | copy-start | bytes 18436
  156.5 286.4 %all-reduce.3.cloned.1.call-start = ((), (), s32[]{:S(2)}) async-start(), calls=%async_computation.4 | async-start | bytes 3145728 | tf_op jit(solution)/shard_map/psum | solution.py:172
  364.2 4.1 slice-start
  365.2 4.3 copy-start.4
  365.2 4.3 copy-start.5
  373.1 7.4 %copy-start.6 = (bf16[512,384]{0,1:T(8,128)(2,1)S(1)}, bf16[512,384]{0,1:T(8,128)(2,1)}, u32[]{:S(2)}) copy-start(bf16[512,384]{0,1:T(8,128)(2,1)} %copy.43) | copy-start | bytes 1179652
  387.3 58.2 %copy-start.10 = (f32[1536]{0:T(1024)S(1)}, f32[1536]{0:T(1024)}, u32[]{:S(2)}) copy-start(f32[1536]{0:T(1024)} %param.17) | copy-start | bytes 18436
  387.3 130.9 %all-reduce.5.cloned.1.call-start = ((), (), s32[]{:S(2)}) async-start(), calls=%async_computation.5 | async-start | bytes 3145728 | tf_op jit(solution)/shard_map/psum | solution.py:178
  442.9 14.8 %slice-start.1 = ((s8[6291456]{0:T(1024)(128)(4,1)}), s8[4194304]{0:T(1024)(128)(4,1)S(1)}, s32[]{:S(2)}) async-start(s8[6291456]{0:T(1024)(128)(4,1)} %bitcast.177), calls=%async_computation.7 | async-start | bytes 8388608
  445.7 12.0 %slice-start.2 = ((s8[6291456]{0:T(1024)(128)(4,1)}), s8[2097152]{0:T(1024)(128)(4,1)S(1)}, s32[]{:S(2)}) async-start(s8[6291456]{0:T(1024)(128)(4,1)} %bitcast.177), calls=%async_computation.8 | async-start | bytes 4194304
  (3 other events, 7.7 us)
Sparse Core Ops, SparseCore 0:
  19.6 122.0 all-gather.4
Sparse Core Ops, SparseCore 1:
  156.6 49.4 all-gather.2
  387.4 55.4 all-reduce.2
  467.0 51.2 all-reduce.4
